TPU v7x, 32 devices: a whole 2x2x4 slice. The times are simulated.
32 devices in a mesh: agent: 8 (over y, x, core), res: 4 (over z).
Axes of the slice: x: 2, y: 2, z: 4, core: 2. Of those that a mesh axis runs over, the one named last changes fastest.
Arguments:
- linear_cost: float32 [2048, 2048], P('agent', 'res'), may hold values from -6 to 6
- agent_type: int32 [2048], P('agent'), may hold values from 0 to 3, as said below
- block_mask: int32 [2048, 16], P('agent', 'res'), may hold values 0 or 1
- inverses: bfloat16 [4, 2048, 2048], P(None, 'res'), as said below
- cost_weight: float32 [2048], P('res'), may hold values from 0.5 to 8
- target: float32 [2048], P('res'), may hold values from -6 to 6
Outputs:
- usage: float32 [2048, 2048], P('agent', 'res')
- shared: float32 [2048], P('res')
- prices: float32 [2048], P('res')
- primal_norm: float32 [5], replicated
- dual_norm: float32 [5], replicated
Inputs may be any that keep to these rules, and one draw needn't show every extreme that they name: Each inverses[k] is exactly symmetric: inverses[k, i, j] equals inverses[k, j, i]. `agent_type`: each aligned block of 256 agents (the agents held by one device along the agent axis) holds exactly 64 agents of each type, in no particular order.
All inputs are finite; a program needn't handle non-finite values. No bound on the sum of `block_mask` on one device may be relied on, other than what follows from the above.
Results may differ from a plain program's by a relative error of at most 0.0039.
Values may be sent and summed in bfloat16 or wider, within the bound.
No kernel may reach another device: no remote copies, remote signals or barrier semaphores. Data moves between devices by JAX's collectives and lax.ppermute only.
A program may use at most 64 MiB of HBM per device.

v0:
```python
import jax
import jax.numpy as jnp
from jax import lax
from jax.sharding import PartitionSpec as P

BLK = 128
ITERS = 5
penalty = 1.0
eps = 1e-06


def on_device(linear_cost, agent_type, block_mask, inverses, cost_weight, target):
    local_agents, local_width = linear_cost.shape
    type_count = inverses.shape[0]
    group_rows = local_agents // type_count
    count = local_agents * lax.axis_size("agent")
    block_count = block_mask.shape[1]
    order = jnp.argsort(agent_type, stable=True)
    restore = jnp.argsort(order, stable=True)
    expand = jnp.broadcast_to(
        block_mask.astype(jnp.float32)[:, :, None], (local_agents, block_count, BLK)
    ).reshape(local_agents, local_width)
    usage = jnp.zeros(linear_cost.shape, jnp.float32)
    mean_usage = jnp.zeros((local_width,), jnp.float32)
    shared = jnp.zeros((local_width,), jnp.float32)
    prices = jnp.zeros((local_width,), jnp.float32)
    primal_list = []
    dual_list = []
    for iteration in range(ITERS):
        rhs = (penalty * (usage - mean_usage + shared - prices) - linear_cost).astype(jnp.bfloat16)
        grouped = rhs[order].reshape(type_count, group_rows, local_width)
        product = jnp.einsum(
            "tas,tws->taw",
            lax.all_gather(grouped, "res", axis=2, tiled=True),
            inverses,
            preferred_element_type=jnp.float32,
        )
        new_usage = product.reshape(local_agents, local_width)[restore]
        new_usage = new_usage * expand
        change_local = penalty * penalty * jnp.sum((new_usage - usage) ** 2)
        usage = new_usage
        column_sum = jnp.sum(usage, axis=0)
        usage_sum = lax.psum(column_sum, "agent")
        dual2 = lax.psum(change_local, ("agent", "res"))
        mean_usage = usage_sum / count
        shared = (cost_weight * target + penalty * (prices + mean_usage)) / (cost_weight + penalty)
        prices = prices + mean_usage - shared
        primal2 = lax.psum(count * jnp.sum((mean_usage - shared) ** 2), "res")
        primal_list.append(jnp.sqrt(primal2 + eps))
        dual_list.append(jnp.sqrt(dual2 + eps))
    primal_norm = jnp.stack(primal_list)
    dual_norm = jnp.stack(dual_list)
    return (usage, shared, prices, primal_norm, dual_norm)


def solution(mesh):
    placed = (
        P("agent", "res"),
        P("agent"),
        P("agent", "res"),
        P(None, "res", None),
        P("res"),
        P("res"),
    )
    return jax.shard_map(
        on_device,
        mesh=mesh,
        in_specs=placed,
        out_specs=(P("agent", "res"), P("res"), P("res"), P(), P()),
        check_vma=False,
    )
```

profile of v0, /device:TPU:12, one launch (start us, length us, event | category | flops | bytes accessed | tf_op | source)
XLA Modules:
  0.0 334.9 jit_solution(6932095263842248031)
XLA Ops:
  7.2 3.8 %sort.31 = (s32[256]{0:T(256)}, s32[256]{0:T(256)S(1)}) sort(s32[256]{0:T(256)} %param.7, s32[256]{0:T(256)S(1)} %iota.7), dimensions={0}, to_apply=%region_0.0 | sort | flops 2048 | bytes 4096 | tf_op jit(solution)/shard_map/jit(argsort)/sort | solution.py:18
  11.1 1.1 subtract_convert_fusion.4
  12.2 1.9 gather_fusion
  14.1 3.2 sort.32
  18.2 25.1 %all-gather.6.cloned.1.call-done = bf16[4,64,2048]{2,1,0:T(8,128)(2,1)} async-done(((bf16[4,64,512]{2,1,0:T(8,128)(2,1)}), bf16[4,64,2048]{2,1,0:T(8,128)(2,1)}) %all-gather.6.cloned.1.call-update) | async-done | bytes 1048592 | tf_op jit(solution)/shard_map/all_gather | solution.py:34
  43.3 6.4 %fusion.13 = f32[4,64,512]{2,1,0:T(8,128)S(1)} fusion(bf16[4,64,2048]{2,1,0:T(8,128)(2,1)} %all-gather.6.cloned.1.call-done, bf16[4,512,2048]{2,1,0:T(8,128)(2,1)} %param.9), kind=kOutput, calls=%fused_computation.56 | convolution fusion | flops 536870912 | bytes 9961472 | tf_op jit(solution)/shard_map/tas,tws->taw/dot_general | solution.py:32
  49.7 1.0 gather_fusion.1
  51.1 11.9 %psum.105 = f32[512]{0:T(512)S(1)} all-reduce(f32[512]{0:T(512)S(1)} %get-tuple-element.44), channel_id=1, replica_groups=mesh['agent'=8,'res'=4] {'agent'}, use_global_device_ids=true, to_apply=%region_3.4 | all-reduce | flops 512 | bytes 4096 | tf_op jit(solution)/shard_map/psum | solution.py:43
  63.7 1.9 gather_fusion.2
  65.7 27.5 %all-gather.8.cloned.1.call-done = bf16[4,64,2048]{2,1,0:T(8,128)(2,1)} async-done(((bf16[4,64,512]{2,1,0:T(8,128)(2,1)}), bf16[4,64,2048]{2,1,0:T(8,128)(2,1)}) %all-gather.8.cloned.1.call-update) | async-done | bytes 1048592 | tf_op jit(solution)/shard_map/all_gather | solution.py:34
  93.1 6.4 %fusion.14 = f32[4,64,512]{2,1,0:T(8,128)S(1)} fusion(bf16[4,64,2048]{2,1,0:T(8,128)(2,1)} %all-gather.8.cloned.1.call-done, bf16[4,512,2048]{2,1,0:T(8,128)(2,1)} %param.9), kind=kOutput, calls=%fused_computation.57 | convolution fusion | flops 536870912 | bytes 9961472 | tf_op jit(solution)/shard_map/tas,tws->taw/dot_general | solution.py:32
  99.5 1.0 gather_fusion.3
  100.6 11.9 %psum.106 = f32[512]{0:T(512)S(1)} all-reduce(f32[512]{0:T(512)S(1)} %get-tuple-element.42), channel_id=1, replica_groups=mesh['agent'=8,'res'=4] {'agent'}, use_global_device_ids=true, to_apply=%region_5.6 | all-reduce | flops 512 | bytes 4096 | tf_op jit(solution)/shard_map/psum | solution.py:43
  113.2 1.9 gather_fusion.4
  115.1 27.5 %all-gather.10.cloned.1.call-done = bf16[4,64,2048]{2,1,0:T(8,128)(2,1)} async-done(((bf16[4,64,512]{2,1,0:T(8,128)(2,1)}), bf16[4,64,2048]{2,1,0:T(8,128)(2,1)}) %all-gather.10.cloned.1.call-update) | async-done | bytes 1048592 | tf_op jit(solution)/shard_map/all_gather | solution.py:34
  142.6 6.4 %fusion.15 = f32[4,64,512]{2,1,0:T(8,128)S(1)} fusion(bf16[4,64,2048]{2,1,0:T(8,128)(2,1)} %all-gather.10.cloned.1.call-done, bf16[4,512,2048]{2,1,0:T(8,128)(2,1)} %param.9), kind=kOutput, calls=%fused_computation.58 | convolution fusion | flops 536870912 | bytes 9961472 | tf_op jit(solution)/shard_map/tas,tws->taw/dot_general | solution.py:32
  148.9 1.0 gather_fusion.5
  150.0 12.1 %psum.107 = f32[512]{0:T(512)S(1)} all-reduce(f32[512]{0:T(512)S(1)} %get-tuple-element.40), channel_id=1, replica_groups=mesh['agent'=8,'res'=4] {'agent'}, use_global_device_ids=true, to_apply=%region_7.8 | all-reduce | flops 512 | bytes 4096 | tf_op jit(solution)/shard_map/psum | solution.py:43
  162.8 1.9 gather_fusion.6
  164.8 27.4 %all-gather.12.cloned.1.call-done = bf16[4,64,2048]{2,1,0:T(8,128)(2,1)} async-done(((bf16[4,64,512]{2,1,0:T(8,128)(2,1)}), bf16[4,64,2048]{2,1,0:T(8,128)(2,1)}) %all-gather.12.cloned.1.call-update) | async-done | bytes 1048592 | tf_op jit(solution)/shard_map/all_gather | solution.py:34
  192.2 6.4 %fusion.16 = f32[4,64,512]{2,1,0:T(8,128)S(1)} fusion(bf16[4,64,2048]{2,1,0:T(8,128)(2,1)} %all-gather.12.cloned.1.call-done, bf16[4,512,2048]{2,1,0:T(8,128)(2,1)} %param.9), kind=kOutput, calls=%fused_computation.59 | convolution fusion | flops 536870912 | bytes 9961472 | tf_op jit(solution)/shard_map/tas,tws->taw/dot_general | solution.py:32
  198.6 1.8 gather_fusion.7
  200.4 1.2 fusion.9
  201.5 11.9 %psum.108 = f32[512]{0:T(512)S(1)} all-reduce(f32[512]{0:T(512)S(1)} %get-tuple-element.38), channel_id=1, replica_groups=mesh['agent'=8,'res'=4] {'agent'}, use_global_device_ids=true, to_apply=%region_9.10 | all-reduce | flops 512 | bytes 4096 | tf_op jit(solution)/shard_map/psum | solution.py:43
  214.1 1.9 gather_fusion.8
  218.6 24.9 %all-gather.14.cloned.1.call-done = bf16[4,64,2048]{2,1,0:T(8,128)(2,1)} async-done(((bf16[4,64,512]{2,1,0:T(8,128)(2,1)}), bf16[4,64,2048]{2,1,0:T(8,128)(2,1)}) %all-gather.14.cloned.1.call-update) | async-done | bytes 1048592 | tf_op jit(solution)/shard_map/all_gather | solution.py:34
  243.5 6.4 %fusion.17 = f32[4,64,512]{2,1,0:T(8,128)S(1)} fusion(bf16[4,64,2048]{2,1,0:T(8,128)(2,1)} %all-gather.14.cloned.1.call-done, bf16[4,512,2048]{2,1,0:T(8,128)(2,1)} %param.9), kind=kOutput, calls=%fused_computation.60 | convolution fusion | flops 536870912 | bytes 9961472 | tf_op jit(solution)/shard_map/tas,tws->taw/dot_general | solution.py:32
  249.9 1.8 gather_fusion.9
  251.7 2.8 multiply_reduce_fusion
  254.5 11.9 %psum.109 = f32[512]{0:T(512)S(1)} all-reduce(f32[512]{0:T(512)S(1)} %get-tuple-element.14), channel_id=1, replica_groups=mesh['agent'=8,'res'=4] {'agent'}, use_global_device_ids=true, to_apply=%region_11.12 | all-reduce | flops 512 | bytes 4096 | tf_op jit(solution)/shard_map/psum | solution.py:43
  268.2 9.8 %all-reduce.1 = (f32[]{:T(128)}, f32[]{:T(128)}, f32[]{:T(128)}, f32[]{:T(128)}, f32[]{:T(128)}) all-reduce(f32[]{:T(128)S(6)} %mul.99, f32[]{:T(128)S(6)} %mul.100, f32[]{:T(128)S(6)} %mul.101, f32[]{:T(128)S(6)} %mul.102, f32[]{:T(128)S(6)} %mul.103), channel_id=1, replica_groups=mesh['agent'=8,'res'=4] {'res'}, use_global_device_ids=true, to_apply=%region_13.14 | all-reduce | flops 5 | bytes 40 | tf_op jit(solution)/shard_map/psum | solution.py:48
  281.3 42.5 %all-reduce = (f32[]{:T(128)}, f32[]{:T(128)}, f32[]{:T(128)}, f32[]{:T(128)}, f32[]{:T(128)}) all-reduce(f32[]{:T(128)} %get-tuple-element.13, f32[]{:T(128)} %get-tuple-element.12, f32[]{:T(128)} %get-tuple-element.11, f32[]{:T(128)} %get-tuple-element.10, f32[]{:T(128)} %get-tuple-element.9), channel_id=1, replica_groups=mesh['agent'=8,'res'=4] {'agent','res'}, use_global_device_ids=true, to_apply=%region_23.24 | all-reduce | flops 5 | bytes 40 | tf_op jit(solution)/shard_map/psum | solution.py:44
  (45 shorter events, 7.2 us)
Async XLA Ops:
  7.2 36.1 %all-gather.6.cloned.1.call-start = ((), (), s32[]{:S(2)}) async-start(), calls=%async_computation | async-start | bytes 1310720 | tf_op jit(solution)/shard_map/all_gather | solution.py:34
  14.0 79.1 %all-gather.8.cloned.1.call-start = ((), (), s32[]{:S(2)}) async-start(), calls=%async_computation.1 | async-start | bytes 1310720 | tf_op jit(solution)/shard_map/all_gather | solution.py:34
  18.1 44.9 %copy-start.1 = (f32[512]{0:T(512)S(1)}, f32[512]{0:T(512)}, u32[]{:S(2)}) copy-start(f32[512]{0:T(512)} %param.10) | copy-start | bytes 6148
  18.1 44.9 %copy-start.3 = (f32[512]{0:T(512)S(1)}, f32[512]{0:T(512)}, u32[]{:S(2)}) copy-start(f32[512]{0:T(512)} %param.11) | copy-start | bytes 6148
  18.1 45.5 %copy-start = (f32[256,512]{1,0:T(8,128)S(1)}, f32[256,512]{1,0:T(8,128)}, u32[]{:S(2)}) copy-start(f32[256,512]{1,0:T(8,128)} %param.6) | copy-start | bytes 1572868
  65.6 77.0 %all-gather.10.cloned.1.call-start = ((), (), s32[]{:S(2)}) async-start(), calls=%async_computation.2 | async-start | bytes 1310720 | tf_op jit(solution)/shard_map/all_gather | solution.py:34
  115.1 77.2 %all-gather.12.cloned.1.call-start = ((), (), s32[]{:S(2)}) async-start(), calls=%async_computation.3 | async-start | bytes 1310720 | tf_op jit(solution)/shard_map/all_gather | solution.py:34
  164.7 78.8 %all-gather.14.cloned.1.call-start = ((), (), s32[]{:S(2)}) async-start(), calls=%async_computation.4 | async-start | bytes 1310720 | tf_op jit(solution)/shard_map/all_gather | solution.py:34
  267.0 61.4 %copy-start.2 = (f32[512]{0:T(512)}, f32[512]{0:T(512)S(1)}, u32[]{:S(2)}) copy-start(f32[512]{0:T(512)S(1)} %get-tuple-element.26) | copy-start | bytes 6148
Sparse Core Ops, SparseCore 0:
  14.2 29.0 all-gather.5
  65.7 27.3 all-gather.7
  115.2 27.3 all-gather.9
  164.8 27.3 all-gather.11
  216.1 27.3 all-gather.13
where the time goes:
time: 336 us; the launch traced here: 335 us
  waiting for transfers between devices  132 us (39%)
  blocking collectives  112 us (33%)
  matrix products  31.9 us (9%)
  between operations  23.8 us (7%)
  local copies, waits for them, and re-layouts  17.4 us (5%)
  other arithmetic  17.3 us (5%)
    all_gather x5, waiting for transfers between devices, on_device(): lax.all_gather(grouped, 'res', axis=2, tiled=True)  132 us
    psum x5, blocking collectives, on_device(): usage_sum = lax.psum(column_sum, 'agent')  59.6 us
    psum x1, blocking collectives, on_device(): dual2 = lax.psum(change_local, ('agent', 'res'))  42.5 us
    dot_general x5, matrix products, on_device(): jnp.einsum('tas,tws->taw', lax.all_gather(grouped, 'res', axis=2, tiled=T...  31.9 us
    psum x1, blocking collectives, on_device(): primal2 = lax.psum(count * jnp.sum((mean_usage - shared) ** 2), 'res')  9.78 us
    gather x5, local copies, waits for them, and re-layouts, on_device(): grouped = rhs[order].reshape(type_count, group_rows, local_width)  9.27 us
  transfers between devices with their start and end apart: 5, of which 5 were waited for; matrix products, arithmetic and copies ran while one was open for 1% of the time, Pallas kernels for 0%

commit v1 on v0

--- a/solution.py
+++ b/solution.py
@@ -7,6 +7,11 @@
 ITERS = 5
 penalty = 1.0
 eps = 1e-06
+
+
+def gather_and_add(block, mesh_axis):
+    terms = lax.all_gather(block, mesh_axis)
+    return jnp.sum(terms, axis=0)
 
 
 def on_device(linear_cost, agent_type, block_mask, inverses, cost_weight, target):
@@ -40,7 +45,7 @@
         change_local = penalty * penalty * jnp.sum((new_usage - usage) ** 2)
         usage = new_usage
         column_sum = jnp.sum(usage, axis=0)
-        usage_sum = lax.psum(column_sum, "agent")
+        usage_sum = gather_and_add(column_sum, "agent")
         dual2 = lax.psum(change_local, ("agent", "res"))
         mean_usage = usage_sum / count
         shared = (cost_weight * target + penalty * (prices + mean_usage)) / (cost_weight + penalty)

time: 336 us -> 319 us (0.949); the launches traced: 335 us -> 314 us
  blocking collectives: 112 us -> 94.6 us
    psum x5 -> x0, blocking collectives: 59.6 us -> none  [on_device(): usage_sum = lax.psum(column_sum, 'agent')]
    all_gather x0 -> x5, blocking collectives: none -> 43.6 us  [gather_and_add(): terms = lax.all_gather(block, mesh_axis)]
    all_gather x5, waiting for transfers between devices: 132 us -> 129 us  [on_device(): lax.all_gather(grouped, 'res', axis=2, tiled=True)]
where the time goes in v1:
time: 319 us; the launch traced here: 314 us
  waiting for transfers between devices  129 us (40%)
  blocking collectives  94.6 us (30%)
  matrix products  31.9 us (10%)
  between operations  23.9 us (7%)
  local copies, waits for them, and re-layouts  17.4 us (5%)
  other arithmetic  17.4 us (5%)
    all_gather x5, waiting for transfers between devices, on_device(): lax.all_gather(grouped, 'res', axis=2, tiled=True)  129 us
    all_gather x5, blocking collectives, gather_and_add(): terms = lax.all_gather(block, mesh_axis)  43.6 us
    psum x1, blocking collectives, on_device(): dual2 = lax.psum(change_local, ('agent', 'res'))  40.6 us
    dot_general x5, matrix products, on_device(): jnp.einsum('tas,tws->taw', lax.all_gather(grouped, 'res', axis=2, tiled=T...  31.9 us
    psum x1, blocking collectives, on_device(): primal2 = lax.psum(count * jnp.sum((mean_usage - shared) ** 2), 'res')  10.3 us
    gather x5, local copies, waits for them, and re-layouts, on_device(): grouped = rhs[order].reshape(type_count, group_rows, local_width)  9.27 us
    gather x5, local copies, waits for them, and re-layouts, on_device(): new_usage = product.reshape(local_agents, local_width)[restore]  6.45 us
  transfers between devices with their start and end apart: 5, of which 5 were waited for; matrix products, arithmetic and copies ran while one was open for 1% of the time, Pallas kernels for 0%

profile of v1, /device:TPU:12, one launch (start us, length us, event | category | flops | bytes accessed | tf_op | source)
XLA Modules:
  0.0 314.3 jit_solution(1774206657027140786)
XLA Ops:
  7.2 3.8 %sort.31 = (s32[256]{0:T(256)}, s32[256]{0:T(256)S(1)}) sort(s32[256]{0:T(256)} %param.7, s32[256]{0:T(256)S(1)} %iota.7), dimensions={0}, to_apply=%region_0.0 | sort | flops 2048 | bytes 4096 | tf_op jit(solution)/shard_map/jit(argsort)/sort | solution.py:23
  11.1 1.1 subtract_convert_fusion.4
  12.2 1.9 gather_fusion
  14.1 3.2 %sort.32 = (s32[256]{0:T(256)}, s32[256]{0:T(256)S(1)}) sort(s32[256]{0:T(256)S(1)} %get-tuple-element.7, s32[256]{0:T(256)S(1)} %iota.8), dimensions={0}, to_apply=%region_1.2 | sort | flops 2048 | bytes 4096 | tf_op jit(solution)/shard_map/jit(argsort)/sort | solution.py:24
  18.2 25.1 %all-gather.16.cloned.1.call-done = bf16[4,64,2048]{2,1,0:T(8,128)(2,1)} async-done(((bf16[4,64,512]{2,1,0:T(8,128)(2,1)}), bf16[4,64,2048]{2,1,0:T(8,128)(2,1)}) %all-gather.16.cloned.1.call-update) | async-done | bytes 1048592 | tf_op jit(solution)/shard_map/all_gather | solution.py:39
  43.3 6.4 %fusion.13 = f32[4,64,512]{2,1,0:T(8,128)S(1)} fusion(bf16[4,64,2048]{2,1,0:T(8,128)(2,1)} %all-gather.16.cloned.1.call-done, bf16[4,512,2048]{2,1,0:T(8,128)(2,1)} %param.9), kind=kOutput, calls=%fused_computation.56 | convolution fusion | flops 536870912 | bytes 9961472 | tf_op jit(solution)/shard_map/tas,tws->taw/dot_general | solution.py:37
  49.7 1.0 gather_fusion.1
  51.1 8.9 %all-gather.5 = f32[8,1,512]{2,1,0:T(1,128)S(1)} all-gather(f32[1,1,512]{2,1,0:T(1,128)S(1)} %bitcast.63), channel_id=2, replica_groups=mesh['agent'=8,'res'=4] {'agent'}, dimensions={0}, use_global_device_ids=true | all-gather | bytes 18432 | tf_op jit(solution)/shard_map/all_gather | solution.py:13
  60.8 1.9 gather_fusion.2
  62.7 26.6 %all-gather.18.cloned.1.call-done = bf16[4,64,2048]{2,1,0:T(8,128)(2,1)} async-done(((bf16[4,64,512]{2,1,0:T(8,128)(2,1)}), bf16[4,64,2048]{2,1,0:T(8,128)(2,1)}) %all-gather.18.cloned.1.call-update) | async-done | bytes 1048592 | tf_op jit(solution)/shard_map/all_gather | solution.py:39
  89.2 6.4 %fusion.14 = f32[4,64,512]{2,1,0:T(8,128)S(1)} fusion(bf16[4,64,2048]{2,1,0:T(8,128)(2,1)} %all-gather.18.cloned.1.call-done, bf16[4,512,2048]{2,1,0:T(8,128)(2,1)} %param.9), kind=kOutput, calls=%fused_computation.57 | convolution fusion | flops 536870912 | bytes 9961472 | tf_op jit(solution)/shard_map/tas,tws->taw/dot_general | solution.py:37
  95.6 1.0 gather_fusion.3
  96.7 8.9 %all-gather.6 = f32[8,1,512]{2,1,0:T(1,128)S(1)} all-gather(f32[1,1,512]{2,1,0:T(1,128)S(1)} %bitcast.64), channel_id=3, replica_groups=mesh['agent'=8,'res'=4] {'agent'}, dimensions={0}, use_global_device_ids=true | all-gather | bytes 18432 | tf_op jit(solution)/shard_map/all_gather | solution.py:13
  106.4 1.9 gather_fusion.4
  108.3 26.6 %all-gather.20.cloned.1.call-done = bf16[4,64,2048]{2,1,0:T(8,128)(2,1)} async-done(((bf16[4,64,512]{2,1,0:T(8,128)(2,1)}), bf16[4,64,2048]{2,1,0:T(8,128)(2,1)}) %all-gather.20.cloned.1.call-update) | async-done | bytes 1048592 | tf_op jit(solution)/shard_map/all_gather | solution.py:39
  134.8 6.4 %fusion.15 = f32[4,64,512]{2,1,0:T(8,128)S(1)} fusion(bf16[4,64,2048]{2,1,0:T(8,128)(2,1)} %all-gather.20.cloned.1.call-done, bf16[4,512,2048]{2,1,0:T(8,128)(2,1)} %param.9), kind=kOutput, calls=%fused_computation.58 | convolution fusion | flops 536870912 | bytes 9961472 | tf_op jit(solution)/shard_map/tas,tws->taw/dot_general | solution.py:37
  141.2 1.0 gather_fusion.5
  142.3 9.0 %all-gather.7 = f32[8,1,512]{2,1,0:T(1,128)S(1)} all-gather(f32[1,1,512]{2,1,0:T(1,128)S(1)} %bitcast.65), channel_id=4, replica_groups=mesh['agent'=8,'res'=4] {'agent'}, dimensions={0}, use_global_device_ids=true | all-gather | bytes 18432 | tf_op jit(solution)/shard_map/all_gather | solution.py:13
  152.1 1.9 gather_fusion.6
  154.1 26.6 %all-gather.22.cloned.1.call-done = bf16[4,64,2048]{2,1,0:T(8,128)(2,1)} async-done(((bf16[4,64,512]{2,1,0:T(8,128)(2,1)}), bf16[4,64,2048]{2,1,0:T(8,128)(2,1)}) %all-gather.22.cloned.1.call-update) | async-done | bytes 1048592 | tf_op jit(solution)/shard_map/all_gather | solution.py:39
  180.6 6.4 %fusion.16 = f32[4,64,512]{2,1,0:T(8,128)S(1)} fusion(bf16[4,64,2048]{2,1,0:T(8,128)(2,1)} %all-gather.22.cloned.1.call-done, bf16[4,512,2048]{2,1,0:T(8,128)(2,1)} %param.9), kind=kOutput, calls=%fused_computation.59 | convolution fusion | flops 536870912 | bytes 9961472 | tf_op jit(solution)/shard_map/tas,tws->taw/dot_general | solution.py:37
  187.0 1.8 gather_fusion.7
  188.8 1.2 fusion.9
  189.9 8.9 %all-gather.8 = f32[8,1,512]{2,1,0:T(1,128)S(1)} all-gather(f32[1,1,512]{2,1,0:T(1,128)S(1)} %bitcast.66), channel_id=5, replica_groups=mesh['agent'=8,'res'=4] {'agent'}, dimensions={0}, use_global_device_ids=true | all-gather | bytes 18432 | tf_op jit(solution)/shard_map/all_gather | solution.py:13
  199.6 1.9 gather_fusion.8
  204.0 24.0 %all-gather.24.cloned.1.call-done = bf16[4,64,2048]{2,1,0:T(8,128)(2,1)} async-done(((bf16[4,64,512]{2,1,0:T(8,128)(2,1)}), bf16[4,64,2048]{2,1,0:T(8,128)(2,1)}) %all-gather.24.cloned.1.call-update) | async-done | bytes 1048592 | tf_op jit(solution)/shard_map/all_gather | solution.py:39
  228.0 6.4 %fusion.17 = f32[4,64,512]{2,1,0:T(8,128)S(1)} fusion(bf16[4,64,2048]{2,1,0:T(8,128)(2,1)} %all-gather.24.cloned.1.call-done, bf16[4,512,2048]{2,1,0:T(8,128)(2,1)} %param.9), kind=kOutput, calls=%fused_computation.60 | convolution fusion | flops 536870912 | bytes 9961472 | tf_op jit(solution)/shard_map/tas,tws->taw/dot_general | solution.py:37
  234.4 1.8 gather_fusion.9
  236.2 2.8 multiply_reduce_fusion
  239.0 40.6 %all-reduce = (f32[]{:T(128)}, f32[]{:T(128)}, f32[]{:T(128)}, f32[]{:T(128)}, f32[]{:T(128)}) all-reduce(f32[]{:T(128)} %get-tuple-element.13, f32[]{:T(128)} %get-tuple-element.12, f32[]{:T(128)} %get-tuple-element.11, f32[]{:T(128)} %get-tuple-element.10, f32[]{:T(128)} %get-tuple-element.9), channel_id=1, replica_groups=mesh['agent'=8,'res'=4] {'agent','res'}, use_global_device_ids=true, to_apply=%region_23.24 | all-reduce | flops 5 | bytes 40 | tf_op jit(solution)/shard_map/psum | solution.py:49
  283.0 8.0 %all-gather.9 = f32[8,1,512]{2,1,0:T(1,128)S(1)} all-gather(f32[1,1,512]{2,1,0:T(1,128)S(1)} %bitcast.62), channel_id=6, replica_groups=mesh['agent'=8,'res'=4] {'agent'}, dimensions={0}, use_global_device_ids=true | all-gather | bytes 18432 | tf_op jit(solution)/shard_map/all_gather | solution.py:13
  292.9 10.3 %all-reduce.1 = (f32[]{:T(128)}, f32[]{:T(128)}, f32[]{:T(128)}, f32[]{:T(128)}, f32[]{:T(128)}) all-reduce(f32[]{:T(128)S(6)} %mul.99, f32[]{:T(128)S(6)} %mul.100, f32[]{:T(128)S(6)} %mul.101, f32[]{:T(128)S(6)} %mul.102, f32[]{:T(128)S(6)} %mul.103), channel_id=1, replica_groups=mesh['agent'=8,'res'=4] {'res'}, use_global_device_ids=true, to_apply=%region_13.14 | all-reduce | flops 5 | bytes 40 | tf_op jit(solution)/shard_map/psum | solution.py:53
  (50 shorter events, 7.3 us)
Async XLA Ops:
  7.2 36.1 %all-gather.16.cloned.1.call-start = ((), (), s32[]{:S(2)}) async-start(), calls=%async_computation | async-start | bytes 1310720 | tf_op jit(solution)/shard_map/all_gather | solution.py:39
  14.0 75.2 %all-gather.18.cloned.1.call-start = ((), (), s32[]{:S(2)}) async-start(), calls=%async_computation.1 | async-start | bytes 1310720 | tf_op jit(solution)/shard_map/all_gather | solution.py:39
  18.1 41.9 %copy-start.1 = (f32[512]{0:T(512)S(1)}, f32[512]{0:T(512)}, u32[]{:S(2)}) copy-start(f32[512]{0:T(512)} %param.10) | copy-start | bytes 6148
  18.1 41.9 %copy-start.3 = (f32[512]{0:T(512)S(1)}, f32[512]{0:T(512)}, u32[]{:S(2)}) copy-start(f32[512]{0:T(512)} %param.11) | copy-start | bytes 6148
  18.1 42.5 %copy-start = (f32[256,512]{1,0:T(8,128)S(1)}, f32[256,512]{1,0:T(8,128)}, u32[]{:S(2)}) copy-start(f32[256,512]{1,0:T(8,128)} %param.6) | copy-start | bytes 1572868
  62.6 72.2 %all-gather.20.cloned.1.call-start = ((), (), s32[]{:S(2)}) async-start(), calls=%async_computation.2 | async-start | bytes 1310720 | tf_op jit(solution)/shard_map/all_gather | solution.py:39
  108.2 72.4 %all-gather.22.cloned.1.call-start = ((), (), s32[]{:S(2)}) async-start(), calls=%async_computation.3 | async-start | bytes 1310720 | tf_op jit(solution)/shard_map/all_gather | solution.py:39
  154.0 74.0 %all-gather.24.cloned.1.call-start = ((), (), s32[]{:S(2)}) async-start(), calls=%async_computation.4 | async-start | bytes 1310720 | tf_op jit(solution)/shard_map/all_gather | solution.py:39
  291.6 16.2 %copy-start.2 = (f32[512]{0:T(512)}, f32[512]{0:T(512)S(1)}, u32[]{:S(2)}) copy-start(f32[512]{0:T(512)S(1)} %get-tuple-element.26) | copy-start | bytes 6148
Sparse Core Ops, SparseCore 0:
  14.2 29.0 all-gather.15
  62.8 26.4 all-gather.17
  108.4 26.4 all-gather.19
  154.1 26.4 all-gather.21
  201.6 26.4 all-gather.23
